TPU v7x, 128 devices: a whole 4x4x4 slice. The times are simulated.
128 devices in a mesh: span: 32 (over x, z, y_lo), ctx: 4 (over y_hi, core).
Axes of the slice: x: 4, y: 4 (y_hi: 2, y_lo: 2; y = y_hi * 2 + y_lo), z: 4, core: 2. Of those that a mesh axis runs over, the one named last changes fastest.
Arguments:
- queries: bfloat16 [16384, 3072], P(('span', 'ctx')), may hold values from -64 to 64
- keys: bfloat16 [16384, 512], P(('span', 'ctx')), may hold values from -16 to 16
- values: bfloat16 [16384, 512], P(('span', 'ctx')), may hold values from -6 to 6
- temps: float32 [8, 24], replicated, may hold values from 0.5 to 2
- levels: int32 [32], replicated, may hold values from 0 to 7
- ctx_list: int32 [32, 4], replicated, may hold values from -1 to 30, as said below
- counts: int32 [32], replicated, may hold values from 256 to 512
Outputs:
- attended: bfloat16 [16384, 3072], P(('span', 'ctx'))
Inputs may be any that keep to these rules, and one draw needn't show every extreme that they name: `ctx_list`: slot 0 of span c's list is c - 1 (-1 for span 0). Slot 1, when used, is span 0. The other slots hold distinct spans below c - 1, used slots first, then -1. The list of span 32 - 1 has no -1.
All inputs are finite; a program needn't handle non-finite values.
Results may differ from a plain program's by a relative error of at most 0.0041.
Values may be sent and summed in bfloat16 or wider, within the bound.
A program may use at most 128 MiB of HBM per device.

v0:
```python
import math
import jax
import jax.numpy as jnp
from jax import lax
from jax.sharding import PartitionSpec as P

HQ = 24
KVH = 4
HD = 128


def slot_scores(query_group, key_slot, scale_group):
    scores = jnp.einsum("rgd,kd->grk", query_group, key_slot, preferred_element_type=jnp.float32)
    return scores * scale_group[:, None, None]


def row_maxima(query_rows, key_slots, mask, scale):
    group_size = HQ // KVH
    row_count = query_rows.shape[0]
    query_heads = query_rows.reshape(row_count, HQ, HD)
    maxima = []
    for kv_head in range(KVH):
        lower = kv_head * group_size
        query_group = query_heads[:, lower : lower + group_size]
        highest = jnp.full((group_size, row_count), -1e30, jnp.float32)
        for slot_index in range(key_slots.shape[0]):
            scores = slot_scores(
                query_group,
                key_slots[slot_index][:, kv_head * HD : (kv_head + 1) * HD],
                scale[lower : lower + group_size],
            )
            scores = jnp.where(mask[slot_index][None, None, :], scores, -1e30)
            highest = jnp.maximum(highest, jnp.max(scores, axis=-1))
        maxima.append(highest)
    return jnp.concatenate(maxima, axis=0)


def weighted_sums(query_rows, key_slots, value_slots, mask, scale, maxima):
    group_size = HQ // KVH
    row_count = query_rows.shape[0]
    query_heads = query_rows.reshape(row_count, HQ, HD)
    sums_list = []
    totals_list = []
    for kv_head in range(KVH):
        lower = kv_head * group_size
        query_group = query_heads[:, lower : lower + group_size]
        highest = maxima[lower : lower + group_size]
        accum = jnp.zeros((row_count, group_size, HD), jnp.float32)
        totals = jnp.zeros((group_size, row_count), jnp.float32)
        for slot_index in range(key_slots.shape[0]):
            scores = slot_scores(
                query_group,
                key_slots[slot_index][:, kv_head * HD : (kv_head + 1) * HD],
                scale[lower : lower + group_size],
            )
            keep = mask[slot_index][None, None, :]
            scores = jnp.where(keep, scores, -1e30)
            weights = jnp.where(keep, jnp.exp(scores - highest[:, :, None]), 0.0)
            totals = totals + jnp.sum(weights, axis=-1)
            value_group = value_slots[slot_index][:, kv_head * HD : (kv_head + 1) * HD]
            accum = accum + jnp.einsum(
                "grk,kd->rgd",
                weights.astype(jnp.bfloat16),
                value_group,
                preferred_element_type=jnp.float32,
            )
        sums_list.append(accum)
        totals_list.append(totals)
    sums = jnp.concatenate(sums_list, axis=1).reshape(row_count, HQ * HD)
    totals = jnp.transpose(jnp.concatenate(totals_list, axis=0))
    return (sums, totals)


def finish(sums, totals):
    row_count = sums.shape[0]
    result = sums.reshape(row_count, HQ, HD) / totals[:, :, None]
    return result.reshape(row_count, HQ * HD).astype(jnp.bfloat16)


def per_device(queries, keys, values, temps, levels, ctx_list, counts):
    span_index = lax.axis_index("span")
    tok_rows = keys.shape[0]
    width = keys.shape[1]
    wanted = lax.dynamic_index_in_dim(ctx_list, span_index, 0, keepdims=False)
    empty = jnp.zeros((wanted.shape[0], tok_rows, width), keys.dtype)
    piece_keys = lax.all_gather(keys, "span", axis=0, tiled=True)
    piece_values = lax.all_gather(values, "span", axis=0, tiled=True)
    length = piece_keys.shape[0]
    new_keys = []
    new_values = []
    for slot_index in range(wanted.shape[0]):
        source = wanted[slot_index]
        offset = source * tok_rows
        inside = (source >= 0) & (offset >= 0) & (offset + tok_rows <= length)
        begin = jnp.clip(offset, 0, length - tok_rows)
        slab_keys = lax.dynamic_slice_in_dim(piece_keys, begin, tok_rows, 0)
        slab_values = lax.dynamic_slice_in_dim(piece_values, begin, tok_rows, 0)
        new_keys.append(lax.select(inside, slab_keys, empty[slot_index]))
        new_values.append(lax.select(inside, slab_values, empty[slot_index]))
    context_keys = jnp.stack(new_keys)
    context_values = jnp.stack(new_values)
    slot_keys = jnp.concatenate([keys[None], context_keys], axis=0)
    slot_values = jnp.concatenate([values[None], context_values], axis=0)
    span_ids = jnp.concatenate([jnp.reshape(span_index, (1,)), wanted])
    valid_span = span_ids >= 0
    lengths = counts[jnp.maximum(span_ids, 0)]
    level = lax.dynamic_index_in_dim(levels, span_index, 0, keepdims=False)
    scale = lax.dynamic_index_in_dim(temps, level, 0, keepdims=False) / math.sqrt(HD)
    all_keys, all_values = (
        lax.all_gather(slot_keys, "ctx", axis=1, tiled=True),
        lax.all_gather(slot_values, "ctx", axis=1, tiled=True),
    )
    positions = jnp.arange(all_keys.shape[1], dtype=jnp.int32)
    mask = valid_span[:, None] & (positions[None, :] < lengths[:, None])
    maxima = row_maxima(queries, all_keys, mask, scale)
    sums, totals = weighted_sums(queries, all_keys, all_values, mask, scale, maxima)
    return finish(sums, totals)


def solution(mesh):
    return jax.shard_map(
        per_device,
        mesh=mesh,
        in_specs=(
            P(("span", "ctx"), None),
            P(("span", "ctx"), None),
            P(("span", "ctx"), None),
            P(),
            P(),
            P(),
            P(),
        ),
        out_specs=P(("span", "ctx"), None),
        check_vma=False,
    )
```

profile of v0, /device:TPU:1, one launch (start us, length us, event | category | flops | bytes accessed | tf_op | source)
XLA Modules:
  0.0 432.0 jit_solution(16926289602360051760)
XLA Ops:
  6.5 0.7 all-gather.9.cloned.1.call-update
  7.3 0.7 all-gather.5.cloned.1.call-update
  8.1 0.9 fusion.212
  8.9 0.5 fusion.213
  14.5 0.9 bitcast_dynamic-update-slice_fusion.4
  15.4 0.9 bitcast_dynamic-update-slice_fusion.9
  16.3 133.3 %all-gather.9.cloned.1.call-done = bf16[4096,512]{1,0:T(8,128)(2,1)} async-done(((bf16[128,512]{1,0:T(8,128)(2,1)}), bf16[4096,512]{1,0:T(8,128)(2,1)}) %all-gather.9.cloned.1.call-update) | async-done | bytes 4194320 | tf_op jit(solution)/shard_map/all_gather | solution.py:86
  149.6 159.8 %all-gather.5.cloned.1.call-done = bf16[4096,512]{1,0:T(8,128)(2,1)} async-done(((bf16[128,512]{1,0:T(8,128)(2,1)}), bf16[4096,512]{1,0:T(8,128)(2,1)}) %all-gather.5.cloned.1.call-update) | async-done | bytes 4194320 | tf_op jit(solution)/shard_map/all_gather | solution.py:87
  309.5 1.1 bitcast_dynamic-update-slice_fusion.3
  310.5 1.0 bitcast_dynamic-update-slice_fusion.2
  311.5 1.0 bitcast_dynamic-update-slice_fusion.1
  312.5 1.0 bitcast_dynamic-update-slice_fusion
  313.4 0.8 copy-done.20
  314.3 0.7 dynamic_slice.45
  317.6 0.6 gather_fusion
  318.3 0.7 fusion.190
  319.2 1.0 bitcast_dynamic-update-slice_fusion.7
  320.2 1.0 bitcast_dynamic-update-slice_fusion.6
  321.1 1.0 bitcast_dynamic-update-slice_fusion.5
  322.1 0.8 copy-done.21
  322.9 42.3 %all-gather.11.cloned.1.call-done = bf16[5,512,512]{2,1,0:T(8,128)(2,1)} async-done(((bf16[5,128,512]{2,1,0:T(8,128)(2,1)}), bf16[5,512,512]{2,1,0:T(8,128)(2,1)}) %all-gather.11.cloned.1.call-update) | async-done | bytes 2621456 | tf_op jit(solution)/shard_map/all_gather | solution.py:110
  365.3 1.9 slice_bitcast_fusion.7
  367.2 1.5 bitcast_reduce_fusion.19
  369.1 1.5 bitcast_reduce_fusion.18
  370.6 1.5 bitcast_reduce_fusion.17
  372.1 1.5 bitcast_reduce_fusion.16
  373.7 1.6 bitcast_reduce_fusion.15
  375.3 1.5 bitcast_reduce_fusion.13
  376.8 1.6 bitcast_reduce_fusion.12
  378.3 1.6 bitcast_reduce_fusion.11
  379.9 1.6 bitcast_reduce_fusion.10
  381.5 1.5 bitcast_reduce_fusion.9
  383.0 1.5 bitcast_reduce_fusion.8
  384.6 1.5 bitcast_reduce_fusion.4
  386.1 1.6 bitcast_reduce_fusion.3
  387.6 1.5 bitcast_reduce_fusion.7
  389.2 1.5 bitcast_reduce_fusion.2
  390.7 1.5 bitcast_reduce_fusion.6
  392.2 1.5 bitcast_reduce_fusion.1
  393.7 1.6 bitcast_reduce_fusion
  395.3 1.5 bitcast_reduce_fusion.5
  396.8 2.1 slice_bitcast_fusion
  399.0 0.4 fusion.107
  399.5 0.8 copy-done.3
  401.0 0.5 convolution_add_fusion.15
  401.5 0.8 copy-done.16
  403.0 0.5 convolution_add_fusion.14
  403.5 0.7 copy-done.17
  405.0 0.5 convolution_add_fusion.13
  405.5 0.7 copy-done.19
  406.6 0.6 copy-done.14
  407.2 3.4 fusion.73
  410.6 0.5 fusion.84
  411.1 0.5 fusion.81
  412.0 0.9 copy-done.4
  413.5 0.4 convolution_add_fusion.10
  414.0 0.8 copy-done.6
  416.0 0.8 copy-done.1
  416.7 0.5 fusion.95
  417.5 0.5 convolution_add_fusion.7
  417.9 0.7 copy-done.9
  419.1 0.6 copy-done.10
  419.7 3.4 fusion.63
  424.3 1.2 copy.94
  (72 shorter events, 8.0 us)
Async XLA Ops:
  6.5 311.1 %copy-start = (s32[32]{0:T(128)S(1)}, s32[32]{0:T(128)}, u32[]{:S(2)}) copy-start(s32[32]{0:T(128)} %param.13) | copy-start | bytes 388
  6.5 307.8 %copy-start.23 = (s32[32]{0:T(128)S(1)}, s32[32]{0:T(128)}, u32[]{:S(2)}) copy-start(s32[32]{0:T(128)} %param.11) | copy-start | bytes 388
  6.5 309.9 %copy-start.22 = (bf16[128,3072]{1,0:T(8,128)(2,1)S(1)}, bf16[128,3072]{1,0:T(8,128)(2,1)}, u32[]{:S(2)}) copy-start(bf16[128,3072]{1,0:T(8,128)(2,1)} %param.7) | copy-start | bytes 2359300
  6.5 143.1 %all-gather.9.cloned.1.call-start = ((), (), s32[]{:S(2)}) async-start(), calls=%async_computation.2 | async-start | bytes 4325376 | tf_op jit(solution)/shard_map/all_gather | solution.py:86
  7.3 302.2 %all-gather.5.cloned.1.call-start = ((), (), s32[]{:S(2)}) async-start(), calls=%async_computation | async-start | bytes 4325376 | tf_op jit(solution)/shard_map/all_gather | solution.py:87
  8.0 357.2 %all-gather.11.cloned.1.call-start = ((), (), s32[]{:S(2)}) async-start(), calls=%async_computation.3 | async-start | bytes 3276800 | tf_op jit(solution)/shard_map/all_gather | solution.py:110
  313.4 0.8 copy-start.20
  314.3 82.6 %all-gather.7.cloned.1.call-start = ((), (), s32[]{:S(2)}) async-start(), calls=%async_computation.1 | async-start | bytes 3276800 | tf_op jit(solution)/shard_map/all_gather | solution.py:111
  322.1 0.8 copy-start.21
  396.8 2.2 copy-start.2
  398.9 1.4 copy-start.3
  399.5 1.5 copy-start.12
  400.8 1.5 copy-start.16
  401.5 1.5 copy-start.13
  402.7 1.5 copy-start.17
  403.5 1.5 copy-start.15
  404.7 1.5 copy-start.19
  405.0 1.6 copy-start.18
  405.5 1.7 copy-start.14
  411.5 1.4 copy-start.4
  412.0 1.5 copy-start.5
  413.4 1.4 copy-start.6
  414.0 1.5 copy-start.7
  415.3 1.5 copy-start.1
  415.9 1.5 copy-start.8
  417.2 1.5 copy-start.9
  417.5 1.6 copy-start.11
  417.9 1.8 copy-start.10
Sparse Core Ops, SparseCore 0:
  9.0 140.5 all-gather.8
  151.3 158.1 all-gather.4
  314.4 50.8 all-gather.10
  366.8 28.9 all-gather.6
where the time goes:
time: 433 us; the launch traced here: 432 us
  waiting for transfers between devices  337 us (78%)
  matrix products  38.6 us (9%)
  local copies, waits for them, and re-layouts  20.9 us (5%)
  between operations  20.7 us (5%)
  other arithmetic  14.8 us (3%)
    all_gather x1, waiting for transfers between devices, per_device(): piece_values = lax.all_gather(values, 'span', axis=0, tiled=True)  160 us
    all_gather x1, waiting for transfers between devices, per_device(): piece_keys = lax.all_gather(keys, 'span', axis=0, tiled=True)  133 us
    all_gather x1, waiting for transfers between devices, per_device(): lax.all_gather(slot_keys, 'ctx', axis=1, tiled=True)  42.3 us
    dot_general x20, matrix products, slot_scores(): jnp.einsum('rgd,kd->grk', query_group, key_slot, preferred_element_type=j...  29.6 us
    unnamed x51, local copies, waits for them, and re-layouts  12.9 us
    dot_general x20, matrix products, weighted_sums(): jnp.einsum('grk,kd->rgd', weights.astype(jnp.bfloat16), value_group, pref...  8.94 us
  transfers between devices with their start and end apart: 4, of which 3 were waited for; matrix products, arithmetic and copies ran while one was open for 9% of the time, Pallas kernels for 0%

commit v1 on v0

--- a/solution.py
+++ b/solution.py
@@ -84,7 +84,9 @@
     wanted = lax.dynamic_index_in_dim(ctx_list, span_index, 0, keepdims=False)
     empty = jnp.zeros((wanted.shape[0], tok_rows, width), keys.dtype)
     piece_keys = lax.all_gather(keys, "span", axis=0, tiled=True)
-    piece_values = lax.all_gather(values, "span", axis=0, tiled=True)
+    piece_values = jnp.concatenate(
+        lax.all_to_all(jnp.stack([values] * lax.axis_size("span")), "span", 0, 0), axis=0
+    )
     length = piece_keys.shape[0]
     new_keys = []
     new_values = []

time: 433 us -> 314 us (0.73)
  waiting for transfers between devices: 337 us -> 207 us
  starting transfers between devices: 0.12 us -> 10.1 us
    all_gather x1 -> x0, waiting for transfers between devices: 160 us -> none  [per_device(): piece_values = lax.all_gather(values, 'span', axis=0, tiled=True)]
    all_to_all x0 -> x1, waiting for transfers between devices: none -> 51.1 us  [per_device(): lax.all_to_all(jnp.stack([values] * lax.axis_size('span')), 'span', 0, 0)]
    all_gather x1, waiting for transfers between devices: 133 us -> 117 us  [per_device(): piece_keys = lax.all_gather(keys, 'span', axis=0, tiled=True)]
    all_to_all x0 -> x1, starting transfers between devices: none -> 9.99 us  [per_device(): lax.all_to_all(jnp.stack([values] * lax.axis_size('span')), 'span', 0, 0)]
    all_gather x1, waiting for transfers between devices: 42.3 us -> 38 us  [per_device(): lax.all_gather(slot_keys, 'ctx', axis=1, tiled=True)]
    unnamed x51 -> x59, local copies, waits for them, and re-layouts: 12.9 us -> 11.1 us
  transfers between devices with their start and end apart: 4 -> 4, of which waited for: 3 -> 3; matrix products, arithmetic and copies ran while one was open for 9% -> 13% of each run, Pallas kernels for 0% -> 0%
where the time goes in v1:
time: 314 us; the launch traced here: 313 us
  waiting for transfers between devices  207 us (66%)
  matrix products  38.6 us (12%)
  local copies, waits for them, and re-layouts  21.9 us (7%)
  between operations  21.1 us (7%)
  other arithmetic  14.9 us (5%)
  starting transfers between devices  10.1 us (3%)
    all_gather x1, waiting for transfers between devices, per_device(): piece_keys = lax.all_gather(keys, 'span', axis=0, tiled=True)  117 us
    all_to_all x1, waiting for transfers between devices, per_device(): lax.all_to_all(jnp.stack([values] * lax.axis_size('span')), 'span', 0, 0)  51.1 us
    all_gather x1, waiting for transfers between devices, per_device(): lax.all_gather(slot_keys, 'ctx', axis=1, tiled=True)  38 us
    dot_general x20, matrix products, slot_scores(): jnp.einsum('rgd,kd->grk', query_group, key_slot, preferred_element_type=j...  29.6 us
    unnamed x59, local copies, waits for them, and re-layouts  11.1 us
    all_to_all x1, starting transfers between devices, per_device(): lax.all_to_all(jnp.stack([values] * lax.axis_size('span')), 'span', 0, 0)  9.99 us
    dot_general x20, matrix products, weighted_sums(): jnp.einsum('grk,kd->rgd', weights.astype(jnp.bfloat16), value_group, pref...  8.96 us
    reduce_sum x2, other arithmetic, weighted_sums(): totals = totals + jnp.sum(weights, axis=-1)  6.85 us
  transfers between devices with their start and end apart: 4, of which 3 were waited for; matrix products, arithmetic and copies ran while one was open for 13% of the time, Pallas kernels for 0%

profile of v1, /device:TPU:1, one launch (start us, length us, event | category | flops | bytes accessed | tf_op | source)
XLA Modules:
  0.0 313.2 jit_solution(7758841934015886435)
XLA Ops:
  6.5 0.7 all-gather.6.cloned.1.call-update
  7.3 3.4 %stack.18 = bf16[32,128,512]{2,1,0:T(8,128)(2,1)} broadcast(bf16[128,512]{1,0:T(8,128)(2,1)} %param.9), dimensions={1,2} | broadcast | bytes 4325376 | tf_op jit(solution)/shard_map/stack | solution.py:88
  10.6 10.0 %all-to-all-start = ((bf16[32,128,512]{2,1,0:T(8,128)(2,1)}), bf16[32,128,512]{2,1,0:T(8,128)(2,1)}, u32[]{:S(2)}, u32[]{:S(2)}) async-start(bf16[32,128,512]{2,1,0:T(8,128)(2,1)} %stack.18), calls=%async_computation | async-start | bytes 8388608 | tf_op jit(solution)/shard_map/all_to_all | solution.py:88
  20.9 0.6 fusion.213
  26.9 51.1 %all-to-all-done = bf16[32,128,512]{2,1,0:T(8,128)(2,1)} async-done(((bf16[32,128,512]{2,1,0:T(8,128)(2,1)}), bf16[32,128,512]{2,1,0:T(8,128)(2,1)}, u32[]{:S(2)}, u32[]{:S(2)}) %all-to-all-start) | async-done | bytes 4194336 | tf_op jit(solution)/shard_map/all_to_all | solution.py:88
  78.0 116.9 %all-gather.6.cloned.1.call-done = bf16[4096,512]{1,0:T(8,128)(2,1)} async-done(((bf16[128,512]{1,0:T(8,128)(2,1)}), bf16[4096,512]{1,0:T(8,128)(2,1)}) %all-gather.6.cloned.1.call-update) | async-done | bytes 4194320 | tf_op jit(solution)/shard_map/all_gather | solution.py:86
  194.9 1.1 bitcast_dynamic-update-slice_fusion.3
  196.0 1.0 bitcast_dynamic-update-slice_fusion.2
  196.9 1.0 bitcast_dynamic-update-slice_fusion.1
  197.9 1.0 bitcast_dynamic-update-slice_fusion
  198.9 0.8 copy-done.21
  199.8 0.7 dynamic_slice.45
  203.0 0.6 gather_fusion
  203.7 0.7 fusion.190
  204.6 1.0 bitcast_dynamic-update-slice_fusion.7
  205.6 1.0 bitcast_dynamic-update-slice_fusion.6
  206.5 1.0 bitcast_dynamic-update-slice_fusion.5
  207.5 0.8 copy-done.22
  208.4 38.0 %all-gather.8.cloned.1.call-done = bf16[5,512,512]{2,1,0:T(8,128)(2,1)} async-done(((bf16[5,128,512]{2,1,0:T(8,128)(2,1)}), bf16[5,512,512]{2,1,0:T(8,128)(2,1)}) %all-gather.8.cloned.1.call-update) | async-done | bytes 2621456 | tf_op jit(solution)/shard_map/all_gather | solution.py:112
  246.3 1.9 slice_bitcast_fusion.7
  248.3 1.5 bitcast_reduce_fusion.3
  249.8 1.5 bitcast_reduce_fusion.8
  251.3 1.6 bitcast_reduce_fusion
  252.9 1.6 bitcast_reduce_fusion.1
  254.5 1.5 bitcast_reduce_fusion.2
  256.0 1.6 bitcast_reduce_fusion.4
  257.7 1.6 bitcast_reduce_fusion.5
  259.2 1.6 bitcast_reduce_fusion.13
  260.8 1.5 bitcast_reduce_fusion.10
  262.3 1.5 bitcast_reduce_fusion.18
  263.8 1.5 bitcast_reduce_fusion.15
  265.3 1.5 bitcast_reduce_fusion.6
  266.8 1.5 bitcast_reduce_fusion.11
  268.3 1.5 bitcast_reduce_fusion.16
  269.9 1.5 bitcast_reduce_fusion.7
  271.8 1.5 bitcast_reduce_fusion.12
  273.3 1.6 bitcast_reduce_fusion.17
  274.9 1.5 bitcast_reduce_fusion.19
  276.4 1.5 bitcast_reduce_fusion.14
  277.9 2.1 slice_bitcast_fusion
  280.6 0.8 copy-done.4
  281.4 0.5 fusion.107
  282.5 0.8 copy-done.18
  283.3 0.5 convolution_add_fusion.15
  284.1 0.5 convolution_add_fusion.2
  284.5 0.7 copy-done.20
  285.3 0.5 convolution_add_fusion.14
  286.0 0.5 convolution_add_fusion.1
  286.5 0.7 copy-done.19
  287.2 0.5 convolution_add_fusion.13
  287.7 0.6 copy-done.13
  288.3 3.4 %fusion.73 = (f32[6,128]{1,0:T(8,128)S(1)}, f32[6,128]{1,0:T(8,128)S(1)}, f32[6,128]{1,0:T(8,128)S(1)}, f32[6,128]{1,0:T(8,128)S(1)}, f32[6,128]{1,0:T(8,128)S(1...) fusion(f32[512,128,6]{1,0,2:T(8,128)S(1)} %copy-done.14, ...), kind=kLoop, calls=%fused_computation.135 | loop fusion | flops 11788800 | bytes 15768064 | tf_op jit(solution)/shard_map/reduce_sum | solution.py:59
  291.7 0.5 fusion.81
  292.2 0.5 fusion.84
  292.6 0.4 fusion.95
  293.1 0.9 copy-done.5
  295.1 0.8 copy-done.10
  297.1 0.8 copy-done.2
  299.1 0.7 copy-done.12
  299.8 0.4 convolution_add_fusion.10
  300.2 0.6 copy-done.6
  300.8 3.4 %fusion.63 = (f32[6,128]{1,0:T(8,128)S(1)}, f32[6,128]{1,0:T(8,128)S(1)}, f32[6,128]{1,0:T(8,128)S(1)}, f32[6,128]{1,0:T(8,128)S(1)}, f32[6,128]{1,0:T(8,128)S(1...) fusion(f32[512,128,6]{1,0,2:T(8,128)S(1)} %copy-done.5, ...), kind=kLoop, calls=%fused_computation.125 | loop fusion | flops 11788800 | bytes 15768064 | tf_op jit(solution)/shard_map/reduce_sum | solution.py:59
  304.7 0.5 fusion.83
  305.5 1.2 copy.94
  (80 shorter events, 7.3 us)
Async XLA Ops:
  6.5 196.5 %copy-start = (s32[32]{0:T(128)S(1)}, s32[32]{0:T(128)}, u32[]{:S(2)}) copy-start(s32[32]{0:T(128)} %param.13) | copy-start | bytes 388
  6.5 188.4 %all-gather.6.cloned.1.call-start = ((), (), s32[]{:S(2)}) async-start(), calls=%async_computation.2 | async-start | bytes 4325376 | tf_op jit(solution)/shard_map/all_gather | solution.py:86
  10.6 10.1 %copy-start.26 = (s32[32,4]{0,1:T(4,128)S(1)}, s32[32,4]{0,1:T(4,128)}, u32[]{:S(2)}) copy-start(s32[32,4]{0,1:T(4,128)} %param.12) | copy-start | bytes 1540
  10.6 16.2 %copy-start.25 = (bf16[128,512]{1,0:T(8,128)(2,1)S(1)}, bf16[128,512]{1,0:T(8,128)(2,1)}, u32[]{:S(2)}) copy-start(bf16[128,512]{1,0:T(8,128)(2,1)} %param.8) | copy-start | bytes 393220
  10.6 16.2 %copy-start.24 = (bf16[128,512]{1,0:T(8,128)(2,1)S(1)}, bf16[128,512]{1,0:T(8,128)(2,1)}, u32[]{:S(2)}) copy-start(bf16[128,512]{1,0:T(8,128)(2,1)} %param.9) | copy-start | bytes 393220
  10.6 67.3 %all-to-all-start = ((bf16[32,128,512]{2,1,0:T(8,128)(2,1)}), bf16[32,128,512]{2,1,0:T(8,128)(2,1)}, u32[]{:S(2)}, u32[]{:S(2)}) async-start(bf16[32,128,512]{2,1,0:T(8,128)(2,1)} %stack.18), calls=%async_computation | async-start | bytes 8388608 | tf_op jit(solution)/shard_map/all_to_all | solution.py:88
  20.6 179.1 %copy-start.27 = (s32[32]{0:T(128)S(1)}, s32[32]{0:T(128)}, u32[]{:S(2)}) copy-start(s32[32]{0:T(128)} %param.11) | copy-start | bytes 388
  20.6 181.2 %copy-start.23 = (bf16[128,3072]{1,0:T(8,128)(2,1)S(1)}, bf16[128,3072]{1,0:T(8,128)(2,1)}, u32[]{:S(2)}) copy-start(bf16[128,3072]{1,0:T(8,128)(2,1)} %param.7) | copy-start | bytes 2359300
  20.6 225.7 %all-gather.8.cloned.1.call-start = ((), (), s32[]{:S(2)}) async-start(), calls=%async_computation.3 | async-start | bytes 3276800 | tf_op jit(solution)/shard_map/all_gather | solution.py:112
  198.8 0.8 copy-start.21
  199.7 78.2 %all-gather.4.cloned.1.call-start = ((), (), s32[]{:S(2)}) async-start(), calls=%async_computation.1 | async-start | bytes 3276800 | tf_op jit(solution)/shard_map/all_gather | solution.py:113
  207.5 0.8 copy-start.22
  277.9 2.2 copy-start.3
  280.0 1.4 copy-start.4
  280.6 1.5 copy-start.14
  281.9 1.5 copy-start.18
  282.5 1.5 copy-start.16
  283.8 1.5 copy-start.20
  284.5 1.5 copy-start.15
  285.7 1.5 copy-start.19
  286.0 1.6 copy-start.17
  286.5 1.8 copy-start.13
  292.6 1.4 copy-start.5
  293.1 1.5 copy-start.11
  294.5 1.4 copy-start.10
  295.1 1.5 copy-start.7
  296.4 1.5 copy-start.2
  297.1 1.5 copy-start.8
  298.3 1.5 copy-start.12
  298.6 1.6 copy-start.9
  299.0 1.8 copy-start.6
  305.2 1.4 copy-start.1
Sparse Core Ops, SparseCore 0:
  9.0 185.8 all-gather.5
  199.8 46.4 all-gather.7
  248.0 29.0 all-gather.3
